TPU v7x, 32 devices: a whole 2x2x4 slice. The times are simulated.
32 devices in a mesh: dp: 4 (over y, x), proto: 4 (over z), pair: 2 (over core).
Axes of the slice: x: 2, y: 2, z: 4, core: 2. Of those that a mesh axis runs over, the one named last changes fastest.
Arguments:
- student_patches: bfloat16 [2, 4096, 256], P('pair', 'dp'), may hold values from -2 to 2
- teacher_patches: bfloat16 [2, 4096, 256], P('pair', 'dp'), may hold values from -8 to 8
- student_proto: bfloat16 [65536, 256], P('proto'), may hold values from -4 to 4
- teacher_proto: bfloat16 [65536, 256], P('proto'), may hold values from -4 to 4
- masked_rows: int32 [2, 1024], P('pair', 'dp'), may hold values from 0 to 1023, as said below
Outputs:
- student_grad: float32 [2, 1024, 256], P('pair', 'dp')
Inputs may be any that keep to these rules, and one draw needn't show every extreme that they name: `masked_rows`: entries of one device's block name distinct patch rows of that device's 4 images (image g owns rows g * 256 to (g + 1) * 256 - 1); every image has between 16 and 112 masked patches.
All inputs are finite; a program needn't handle non-finite values.
Results may differ from a plain program's by a relative error of at most 0.00075.
The roundings to bfloat16 on the way count: a program that leaves them out, or rounds other values in their place, can miss the bound.
Values sent between devices are 32-bit elements; how exact they have to be, the bound alone decides.
No kernel may reach another device: no remote copies, remote signals or barrier semaphores. Data moves between devices by JAX's collectives and lax.ppermute only.
A program may use at most 128 MiB of HBM per device.

v0:
```python
import jax
import jax.numpy as jnp
from jax import lax
from jax.sharding import PartitionSpec as P

PATCHES = 256
ITERS = 2
teacher_temp = 0.07
student_temp = 0.1
epsilon = 1e-06


def inverse_norms(matrix):
    return lax.rsqrt(jnp.sum(jnp.square(matrix.astype(jnp.float32)), axis=-1) + epsilon)


def scores_of(features, protos):
    return lax.dot_general(
        features, protos, (((1,), (1,)), ((), ())), preferred_element_type=jnp.float32
    )


def on_device(student_patches, teacher_patches, student_proto, teacher_proto, masked_rows):
    slot_rows = masked_rows[0]
    count_slots = slot_rows.shape[0]
    images = student_patches.shape[1] // PATCHES
    image_of = slot_rows // PATCHES
    member = (image_of[:, None] == jnp.arange(images, dtype=jnp.int32)[None, :]).astype(jnp.float32)
    per_image = jnp.sum(member, axis=0)
    slot_count = jnp.sum(member * per_image[None, :], axis=1)
    weights = count_slots / images / slot_count
    student_rows = jnp.take(student_patches[0], slot_rows, axis=0)
    teacher_rows = jnp.take(teacher_patches[0], slot_rows, axis=0)
    teacher_scale = inverse_norms(teacher_proto)
    student_scale = inverse_norms(student_proto)
    teacher_inv = inverse_norms(teacher_rows)
    teacher_exp = jnp.exp(
        scores_of(teacher_rows, teacher_proto)
        * teacher_inv[:, None]
        * teacher_scale[None, :]
        / teacher_temp
    )
    row_factor = jnp.ones((count_slots,), jnp.float32)
    column_factor = jnp.ones((teacher_proto.shape[0],), jnp.float32)
    for sweep in range(ITERS):
        column_part = jnp.dot(row_factor, teacher_exp, precision=lax.Precision.HIGHEST)
        column_factor = 1.0 / lax.psum(column_part, ("dp", "pair"))
        row_part = jnp.dot(teacher_exp, column_factor, precision=lax.Precision.HIGHEST)
        row_factor = 1.0 / lax.psum(row_part, "proto")
    targets = (teacher_exp * row_factor[:, None] * (column_factor * student_scale)[None, :]).astype(
        jnp.bfloat16
    )
    student_inv = inverse_norms(student_rows)
    student_exp = jnp.exp(
        scores_of(student_rows, student_proto)
        * student_inv[:, None]
        * student_scale[None, :]
        / student_temp
    )
    partition_part = jnp.sum(student_exp, axis=1)
    partition = lax.psum(partition_part, "proto")
    pushed_w = (student_exp * student_scale[None, :]).astype(jnp.bfloat16)
    pushed = jnp.dot(pushed_w, student_proto, preferred_element_type=jnp.float32)
    pulled = jnp.dot(targets, student_proto, preferred_element_type=jnp.float32)
    pushed, pulled = lax.psum((pushed, pulled), "proto")
    inner_grad = (pushed / partition[:, None] - pulled) / student_temp
    rows_float = student_rows.astype(jnp.float32)
    row_dot = jnp.sum(rows_float * inner_grad, axis=1)
    cube = student_inv * student_inv * student_inv
    result_grad = weights[:, None] * (
        student_inv[:, None] * inner_grad - rows_float * (cube * row_dot)[:, None]
    )
    return result_grad[None]


def solution(mesh):
    placed = (
        P("pair", "dp", None),
        P("pair", "dp", None),
        P("proto", None),
        P("proto", None),
        P("pair", "dp"),
    )
    return jax.shard_map(
        on_device, mesh=mesh, in_specs=placed, out_specs=P("pair", "dp", None), check_vma=False
    )
```

profile of v0, /device:TPU:0, one launch (start us, length us, event | category | flops | bytes accessed | tf_op | source)
XLA Modules:
  0.0 296.8 jit_solution(648709590151249231)
XLA Ops:
  6.5 0.0 copy-start
  6.5 0.0 all-reduce.6.cloned.1.call-start
  6.5 0.7 compare_and_fusion
  7.3 0.7 and_select_fusion
  8.0 5.2 %multiply_reduce_fusion = f32[16384]{0:T(1024)S(1)} fusion(bf16[16384,256]{1,0:T(8,128)(2,1)} %param.10), kind=kLoop, calls=%fused_computation.11 | loop fusion | flops 12566528 | bytes 8454144 | tf_op jit(solution)/shard_map/reduce_sum | solution.py:14
  13.2 0.0 copy-done
  13.2 1.2 gather_fusion
  14.4 2.1 gather_fusion.1
  16.5 0.2 fusion.11
  16.7 12.4 %fusion.2 = f32[256,16384]{1,0:T(8,128)} fusion(bf16[16384,256]{1,0:T(8,128)(2,1)} %param.10, f32[16384]{0:T(1024)S(1)} %add_rsqrt_fusion, f32[256]{0:T(256)S(1)} %add_rsqrt_fusion.2, bf16[256,256]{1,0:T(8,128)(2,1)S(1)} %gather_fusion.1, pred[256]{0:T(512)(128)(4,1)S(1)} %compare_and_fusion), kind=kOutput, calls=%fused_computation.5 | convolution fusion | flops 2160132096 | bytes 25363712 | tf_op jit(solution)/shard_map/dot_general | solution.py:18
  29.1 12.1 %fusion.17 = f32[1,16384]{1,0:T(1,128)} fusion(f32[256,16384]{1,0:T(8,128)} %fusion.2), kind=kOutput, calls=%fused_computation.49 | convolution fusion | flops 50331648 | bytes 16842752 | tf_op jit(solution)/shard_map/dot_general | solution.py:46
  41.1 0.0 all-reduce.6.cloned.1.call-update
  41.2 0.2 all-reduce.8.cloned.1.call-start
  41.4 5.2 %multiply_reduce_fusion.1 = f32[16384]{0:T(1024)S(1)} fusion(bf16[16384,256]{1,0:T(8,128)(2,1)} %param.9), kind=kLoop, calls=%fused_computation.13 | loop fusion | flops 12566528 | bytes 8454144 | tf_op jit(solution)/shard_map/reduce_sum | solution.py:14
  46.6 50.6 %all-reduce.6.cloned.1.call-done = f32[16384]{0:T(1024)} async-done(((f32[16384]{0:T(1024)}), f32[16384]{0:T(1024)}) %all-reduce.6.cloned.1.call-update) | async-done | bytes 65552 | tf_op jit(solution)/shard_map/psum | solution.py:47
  97.2 0.9 broadcast_divide_fusion.1
  98.1 16.1 %fusion.23 = f32[1,256]{1,0:T(1,128)S(1)} fusion(f32[256,16384]{1,0:T(8,128)} %fusion.2, f32[16384,1]{0,1:T(1,128)S(1)} %bitcast.28), kind=kOutput, calls=%fused_computation.59 | convolution fusion | flops 50331648 | bytes 16843776 | tf_op jit(solution)/shard_map/dot_general | solution.py:48
  114.1 11.7 %psum.52 = f32[256]{0:T(256)S(1)} all-reduce(f32[256]{0:T(256)S(1)} %bitcast.30), channel_id=1, replica_groups=mesh['dp'=4,'proto'=4,'pair'=2] {'proto'}, use_global_device_ids=true, to_apply=%region_10.12 | all-reduce | flops 256 | bytes 2048 | tf_op jit(solution)/shard_map/psum | solution.py:49
  125.8 12.1 %fusion.24 = f32[1,16384]{1,0:T(1,128)} fusion(f32[256,1]{0,1:T(1,128)S(1)} %bitcast.31, f32[256,16384]{1,0:T(8,128)} %fusion.2), kind=kOutput, calls=%fused_computation.60 | convolution fusion | flops 50331648 | bytes 16843776 | tf_op jit(solution)/shard_map/dot_general | solution.py:46
  137.9 0.0 all-reduce.8.cloned.1.call-update
  137.9 0.3 all-reduce.10.cloned.1.call-start
  138.2 49.7 %all-reduce.8.cloned.1.call-done = f32[16384]{0:T(1024)} async-done(((f32[16384]{0:T(1024)}), f32[16384]{0:T(1024)}) %all-reduce.8.cloned.1.call-update) | async-done | bytes 65552 | tf_op jit(solution)/shard_map/psum | solution.py:47
  187.9 0.9 add_rsqrt_fusion.1
  188.8 16.1 %fusion.25 = f32[1,256]{1,0:T(1,128)S(1)} fusion(f32[256,16384]{1,0:T(8,128)} %fusion.2, f32[16384,1]{0,1:T(1,128)S(1)} %bitcast.25), kind=kOutput, calls=%fused_computation.61 | convolution fusion | flops 50331648 | bytes 16843776 | tf_op jit(solution)/shard_map/dot_general | solution.py:48
  204.8 12.6 %fusion.22 = (f32[256]{0:T(256)S(1)}, f32[256,16384]{1,0:T(8,128)}) fusion(f32[16384]{0:T(1024)S(1)} %get-tuple-element.12, f32[256]{0:T(256)S(1)} %add_rsqrt_fusion.3, bf16[16384,256]{1,0:T(8,128)(2,1)} %param.9, bf16[256,256]{1,0:T(8,128)(2,1)S(1)} %gather_fusion, pred[256]{0:T(512)(128)(4,1)S(1)} %compare_and_fusion), kind=kOutput, calls=%fused_computation.58 | convolution fusion | flops 2164326144 | bytes 25364736 | tf_op jit(solution)/shard_map/dot_general | solution.py:18
  217.5 11.7 %all-reduce = (f32[256]{0:T(256)S(1)}, f32[256]{0:T(256)S(1)}) all-reduce(f32[256]{0:T(256)S(1)} %bitcast.29, f32[256]{0:T(256)S(1)} %get-tuple-element.19), channel_id=1, replica_groups=mesh['dp'=4,'proto'=4,'pair'=2] {'proto'}, use_global_device_ids=true, to_apply=%region_12.14 | all-reduce | flops 512 | bytes 4096 | tf_op jit(solution)/shard_map/psum | solution.py:49
  229.1 11.2 %fusion.6 = f32[256,256]{1,0:T(8,128)} fusion(bf16[16384,256]{1,0:T(8,128)(2,1)} %param.9, f32[256,16384]{1,0:T(8,128)} %get-tuple-element.20, f32[16384]{0:T(1024)S(1)} %get-tuple-element.12), kind=kOutput, calls=%fused_computation.14 | convolution fusion | flops 2155872256 | bytes 25493504 | tf_op jit(solution)/shard_map/dot_general | solution.py:63
  240.3 11.2 %fusion.7 = f32[256,256]{1,0:T(8,128)} fusion(bf16[16384,256]{1,0:T(8,128)(2,1)} %param.9, f32[256,16384]{1,0:T(8,128)} %fusion.2, f32[16384]{0:T(1024)S(1)} %get-tuple-element.13, f32[256]{0:T(256)S(1)} %broadcast_divide_fusion.3), kind=kOutput, calls=%fused_computation.15 | convolution fusion | flops 2160066560 | bytes 25494528 | tf_op jit(solution)/shard_map/dot_general | solution.py:64
  251.6 0.0 all-reduce.10.cloned.1.call-update
  251.6 0.1 convert_reduce_fusion
  251.7 0.1 select_reduce_fusion
  251.8 35.3 %all-reduce.10.cloned.1.call-done = (f32[256,256]{1,0:T(8,128)}, f32[256,256]{1,0:T(8,128)}) async-done(((f32[256,256]{1,0:T(8,128)}, f32[256,256]{1,0:T(8,128)}), (f32[256,256]{1,0:T(8,128)}, f32[256,256]{1,0:T(8,128)})) %all-reduce.10.cloned.1.call-update) | async-done | bytes 524304 | tf_op jit(solution)/shard_map/psum | solution.py:65
  287.1 1.2 fusion.12
  288.3 2.0 fusion.15
  (8 shorter events, 0.1 us)
Async XLA Ops:
  6.5 6.7 %copy-start = (bf16[1,1024,256]{2,1,0:T(8,128)(2,1)S(1)}, bf16[1,1024,256]{2,1,0:T(8,128)(2,1)}, u32[]{:S(2)}) copy-start(bf16[1,1024,256]{2,1,0:T(8,128)(2,1)} %param.7) | copy-start | bytes 1572868
  6.5 90.7 %all-reduce.6.cloned.1.call-start = ((), (), s32[]{:S(2)}) async-start(), calls=%async_computation | async-start | bytes 131072 | tf_op jit(solution)/shard_map/psum | solution.py:47
  41.2 146.7 %all-reduce.8.cloned.1.call-start = ((), (), s32[]{:S(2)}) async-start(), calls=%async_computation.1 | async-start | bytes 131072 | tf_op jit(solution)/shard_map/psum | solution.py:47
  137.9 149.2 %all-reduce.10.cloned.1.call-start = ((), (), s32[]{:S(2)}) async-start(), calls=%async_computation.2 | async-start | bytes 1048576 | tf_op jit(solution)/shard_map/psum | solution.py:65
Sparse Core Ops, SparseCore 0:
  41.3 55.8 all-reduce.5
  138.0 49.8 all-reduce.7
  251.7 35.3 all-reduce.9
where the time goes:
time: 297 us
  waiting for transfers between devices  136 us (46%)
  matrix products  104 us (35%)
  blocking collectives  23.3 us (8%)
  other arithmetic  17.3 us (6%)
  between operations  13.2 us (4%)
  local copies, waits for them, and re-layouts  3.23 us (1%)
    psum x2, waiting for transfers between devices, on_device(): column_factor = 1.0 / lax.psum(column_part, ('dp', 'pair'))  100 us
    psum x1, waiting for transfers between devices, on_device(): pushed, pulled = lax.psum((pushed, pulled), 'proto')  35.3 us
    dot_general x2, matrix products, on_device(): jnp.dot(teacher_exp, column_factor, precision=lax.Precision.HIGHEST)  32.1 us
    dot_general x2, matrix products, scores_of(): lax.dot_general(features, protos, (((1,), (1,)), ((), ())), preferred_ele...  25 us
    dot_general x2, matrix products, on_device(): jnp.dot(row_factor, teacher_exp, precision=lax.Precision.HIGHEST)  24.1 us
    psum x2, blocking collectives, on_device(): row_factor = 1.0 / lax.psum(row_part, 'proto')  23.3 us
    dot_general x1, matrix products, on_device(): pulled = jnp.dot(targets, student_proto, preferred_element_type=jnp.float32)  11.2 us
    dot_general x1, matrix products, on_device(): jnp.dot(pushed_w, student_proto, preferred_element_type=jnp.float32)  11.2 us
  transfers between devices with their start and end apart: 3, of which 3 were waited for; matrix products, arithmetic and copies ran while one was open for 2% of the time, Pallas kernels for 0%

commit v1 on v0

--- a/solution.py
+++ b/solution.py
@@ -44,7 +44,7 @@
     column_factor = jnp.ones((teacher_proto.shape[0],), jnp.float32)
     for sweep in range(ITERS):
         column_part = jnp.dot(row_factor, teacher_exp, precision=lax.Precision.HIGHEST)
-        column_factor = 1.0 / lax.psum(column_part, ("dp", "pair"))
+        column_factor = 1.0 / jnp.sum(lax.all_gather(column_part, ("dp", "pair")), axis=0)
         row_part = jnp.dot(teacher_exp, column_factor, precision=lax.Precision.HIGHEST)
         row_factor = 1.0 / lax.psum(row_part, "proto")
     targets = (teacher_exp * row_factor[:, None] * (column_factor * student_scale)[None, :]).astype(

time: 297 us -> 214 us (0.72)
  waiting for transfers between devices: 136 us -> 37.3 us
  blocking collectives: 23.3 us -> 41.8 us
    psum x2 -> x0, waiting for transfers between devices: 100 us -> none  [on_device(): column_factor = 1.0 / lax.psum(column_part, ('dp', 'pair'))]
    all_gather x0 -> x2, blocking collectives: none -> 21.5 us  [on_device(): lax.all_gather(column_part, ('dp', 'pair'))]
    psum x2, blocking collectives: 23.3 us -> 20.3 us  [on_device(): row_factor = 1.0 / lax.psum(row_part, 'proto')]
  transfers between devices with their start and end apart: 3 -> 1, of which waited for: 3 -> 1; matrix products, arithmetic and copies ran while one was open for 2% -> 0% of each run, Pallas kernels for 0% -> 0%
where the time goes in v1:
time: 214 us; the launch traced here: 213 us
  matrix products  102 us (48%)
  blocking collectives  41.8 us (20%)
  waiting for transfers between devices  37.3 us (17%)
  other arithmetic  15.9 us (7%)
  between operations  13.5 us (6%)
  local copies, waits for them, and re-layouts  2.51 us (1%)
    psum x1, waiting for transfers between devices, on_device(): pushed, pulled = lax.psum((pushed, pulled), 'proto')  37.3 us
    dot_general x2, matrix products, on_device(): jnp.dot(teacher_exp, column_factor, precision=lax.Precision.HIGHEST)  32.1 us
    dot_general x2, matrix products, scores_of(): lax.dot_general(features, protos, (((1,), (1,)), ((), ())), preferred_ele...  25 us
    dot_general x2, matrix products, on_device(): jnp.dot(row_factor, teacher_exp, precision=lax.Precision.HIGHEST)  22.9 us
    all_gather x2, blocking collectives, on_device(): lax.all_gather(column_part, ('dp', 'pair'))  21.5 us
    psum x2, blocking collectives, on_device(): row_factor = 1.0 / lax.psum(row_part, 'proto')  20.3 us
    dot_general x1, matrix products, on_device(): pulled = jnp.dot(targets, student_proto, preferred_element_type=jnp.float32)  11.2 us
    dot_general x1, matrix products, on_device(): jnp.dot(pushed_w, student_proto, preferred_element_type=jnp.float32)  11.2 us
  transfers between devices with their start and end apart: 1, of which 1 were waited for; matrix products, arithmetic and copies ran while one was open for 0% of the time, Pallas kernels for 0%

profile of v1, /device:TPU:0, one launch (start us, length us, event | category | flops | bytes accessed | tf_op | source)
XLA Modules:
  0.0 213.5 jit_solution(17437117129867329421)
XLA Ops:
  6.5 0.0 copy-start
  6.5 0.0 copy-start.1
  6.5 0.0 all-reduce.4.cloned.1.call-start
  6.5 0.8 compare_and_fusion
  7.3 0.7 and_select_fusion
  8.0 5.2 %multiply_reduce_fusion = f32[16384]{0:T(1024)S(1)} fusion(bf16[16384,256]{1,0:T(8,128)(2,1)} %param.10), kind=kLoop, calls=%fused_computation.11 | loop fusion | flops 12566528 | bytes 8454144 | tf_op jit(solution)/shard_map/reduce_sum | solution.py:14
  13.3 5.2 %multiply_reduce_fusion.1 = f32[16384]{0:T(1024)S(1)} fusion(bf16[16384,256]{1,0:T(8,128)(2,1)} %param.9), kind=kLoop, calls=%fused_computation.13 | loop fusion | flops 12566528 | bytes 8454144 | tf_op jit(solution)/shard_map/reduce_sum | solution.py:14
  18.5 0.0 copy-done
  18.5 1.2 gather_fusion
  19.7 0.0 copy-done.1
  19.7 1.2 gather_fusion.1
  20.8 0.2 fusion.11
  21.1 12.4 %fusion.2 = f32[256,16384]{1,0:T(8,128)} fusion(bf16[16384,256]{1,0:T(8,128)(2,1)} %param.10, f32[16384]{0:T(1024)S(1)} %add_rsqrt_fusion, f32[256]{0:T(256)S(1)} %get-tuple-element.21, bf16[256,256]{1,0:T(8,128)(2,1)S(1)} %gather_fusion.1, pred[256]{0:T(512)(128)(4,1)S(1)} %compare_and_fusion), kind=kOutput, calls=%fused_computation.5 | convolution fusion | flops 2160132096 | bytes 25363712 | tf_op jit(solution)/shard_map/dot_general | solution.py:18
  33.4 11.4 %fusion.17 = f32[1,16384]{1,0:T(1,128)S(1)} fusion(f32[256,16384]{1,0:T(8,128)} %fusion.2), kind=kOutput, calls=%fused_computation.49 | convolution fusion | flops 50331648 | bytes 16842752 | tf_op jit(solution)/shard_map/dot_general | solution.py:46
  44.9 11.5 %all-gather = f32[131072]{0:T(1024)S(1)} all-gather(f32[16384]{0:T(1024)S(1)} %bitcast.27), channel_id=2, replica_groups=mesh['dp'=4,'proto'=4,'pair'=2] {'dp','pair'}, dimensions={0}, use_global_device_ids=true | all-gather | bytes 589824 | tf_op jit(solution)/shard_map/all_gather | solution.py:47
  56.4 0.1 reshape.84
  56.5 0.1 reduce_sum.97
  56.6 16.1 %fusion.23 = f32[1,256]{1,0:T(1,128)S(1)} fusion(f32[256,16384]{1,0:T(8,128)} %fusion.2, f32[16384,1]{0,1:T(1,128)S(1)} %bitcast.28), kind=kOutput, calls=%fused_computation.59 | convolution fusion | flops 50331648 | bytes 16843776 | tf_op jit(solution)/shard_map/dot_general | solution.py:48
  72.7 12.0 %psum.37 = f32[256]{0:T(256)S(1)} all-reduce(f32[256]{0:T(256)S(1)} %bitcast.30), channel_id=1, replica_groups=mesh['dp'=4,'proto'=4,'pair'=2] {'proto'}, use_global_device_ids=true, to_apply=%region_10.12 | all-reduce | flops 256 | bytes 2048 | tf_op jit(solution)/shard_map/psum | solution.py:49
  84.7 11.4 %fusion.24 = f32[1,16384]{1,0:T(1,128)S(1)} fusion(f32[256,1]{0,1:T(1,128)S(1)} %bitcast.31, f32[256,16384]{1,0:T(8,128)} %fusion.2), kind=kOutput, calls=%fused_computation.60 | convolution fusion | flops 50331648 | bytes 16843776 | tf_op jit(solution)/shard_map/dot_general | solution.py:46
  96.1 10.0 %all-gather.1 = f32[131072]{0:T(1024)S(1)} all-gather(f32[16384]{0:T(1024)S(1)} %bitcast.26), channel_id=3, replica_groups=mesh['dp'=4,'proto'=4,'pair'=2] {'dp','pair'}, dimensions={0}, use_global_device_ids=true | all-gather | bytes 589824 | tf_op jit(solution)/shard_map/all_gather | solution.py:47
  106.1 0.1 reshape.85
  106.2 0.1 reduce_sum.98
  106.4 16.1 %fusion.25 = f32[1,256]{1,0:T(1,128)S(1)} fusion(f32[256,16384]{1,0:T(8,128)} %fusion.2, f32[16384,1]{0,1:T(1,128)S(1)} %bitcast.25), kind=kOutput, calls=%fused_computation.61 | convolution fusion | flops 50331648 | bytes 16843776 | tf_op jit(solution)/shard_map/dot_general | solution.py:48
  122.5 12.6 %fusion.22 = (f32[256]{0:T(256)S(1)}, f32[256,16384]{1,0:T(8,128)}) fusion(f32[16384]{0:T(1024)S(1)} %get-tuple-element.12, f32[256]{0:T(256)S(1)} %get-tuple-element.22, bf16[16384,256]{1,0:T(8,128)(2,1)} %param.9, bf16[256,256]{1,0:T(8,128)(2,1)S(1)} %gather_fusion, pred[256]{0:T(512)(128)(4,1)S(1)} %compare_and_fusion), kind=kOutput, calls=%fused_computation.58 | convolution fusion | flops 2164326144 | bytes 25364736 | tf_op jit(solution)/shard_map/dot_general | solution.py:18
  135.1 8.3 %all-reduce = (f32[256]{0:T(256)S(1)}, f32[256]{0:T(256)S(1)}) all-reduce(f32[256]{0:T(256)S(1)} %bitcast.29, f32[256]{0:T(256)S(1)} %get-tuple-element.19), channel_id=1, replica_groups=mesh['dp'=4,'proto'=4,'pair'=2] {'proto'}, use_global_device_ids=true, to_apply=%region_12.14 | all-reduce | flops 512 | bytes 4096 | tf_op jit(solution)/shard_map/psum | solution.py:49
  143.5 11.2 %fusion.6 = f32[256,256]{1,0:T(8,128)} fusion(bf16[16384,256]{1,0:T(8,128)(2,1)} %param.9, f32[256,16384]{1,0:T(8,128)} %get-tuple-element.20, f32[16384]{0:T(1024)S(1)} %get-tuple-element.12), kind=kOutput, calls=%fused_computation.14 | convolution fusion | flops 2155872256 | bytes 25493504 | tf_op jit(solution)/shard_map/dot_general | solution.py:63
  154.7 11.2 %fusion.7 = f32[256,256]{1,0:T(8,128)} fusion(bf16[16384,256]{1,0:T(8,128)(2,1)} %param.9, f32[256,16384]{1,0:T(8,128)} %fusion.2, f32[16384]{0:T(1024)S(1)} %get-tuple-element.13, f32[256]{0:T(256)S(1)} %broadcast_divide_fusion.3), kind=kOutput, calls=%fused_computation.15 | convolution fusion | flops 2160066560 | bytes 25494528 | tf_op jit(solution)/shard_map/dot_general | solution.py:64
  165.9 0.0 all-reduce.4.cloned.1.call-update
  165.9 0.1 convert_reduce_fusion
  166.0 0.1 select_reduce_fusion
  166.1 37.3 %all-reduce.4.cloned.1.call-done = (f32[256,256]{1,0:T(8,128)}, f32[256,256]{1,0:T(8,128)}) async-done(((f32[256,256]{1,0:T(8,128)}, f32[256,256]{1,0:T(8,128)}), (f32[256,256]{1,0:T(8,128)}, f32[256,256]{1,0:T(8,128)})) %all-reduce.4.cloned.1.call-update) | async-done | bytes 524304 | tf_op jit(solution)/shard_map/psum | solution.py:65
  203.4 1.2 fusion.12
  204.7 2.0 fusion.15
  (9 shorter events, 0.1 us)
Async XLA Ops:
  6.5 12.0 %copy-start = (bf16[1,1024,256]{2,1,0:T(8,128)(2,1)S(1)}, bf16[1,1024,256]{2,1,0:T(8,128)(2,1)}, u32[]{:S(2)}) copy-start(bf16[1,1024,256]{2,1,0:T(8,128)(2,1)} %param.7) | copy-start | bytes 1572868
  6.5 13.1 %copy-start.1 = (bf16[1,1024,256]{2,1,0:T(8,128)(2,1)S(1)}, bf16[1,1024,256]{2,1,0:T(8,128)(2,1)}, u32[]{:S(2)}) copy-start(bf16[1,1024,256]{2,1,0:T(8,128)(2,1)} %param.8) | copy-start | bytes 1572868
  6.5 196.9 %all-reduce.4.cloned.1.call-start = ((), (), s32[]{:S(2)}) async-start(), calls=%async_computation | async-start | bytes 1048576 | tf_op jit(solution)/shard_map/psum | solution.py:65
Sparse Core Ops, SparseCore 0:
  166.0 37.3 all-reduce.3
